TPU v7x, 32 devices: a whole 2x2x4 slice. The times are simulated.
32 devices in a mesh: facet: 8 (over y, x, core), col: 4 (over z).
Axes of the slice: x: 2, y: 2, z: 4, core: 2. Of those that a mesh axis runs over, the one named last changes fastest.
Arguments:
- facets: float32 [2, 8, 24, 2, 4096], P(None, 'facet', None, None, 'col'), may hold values from -6 to 6
- facet_x: int32 [8], P('facet'), may hold values from 0 to 32767
- facet_y: int32 [2], replicated, may hold values from 0 to 32767
- col_u: int32 [8], replicated, may hold values from 0 to 32767
- slot_col: int32 [4, 8], P('col'), may hold values from 0 to 1
- slot_v: int32 [4, 8], P('col'), may hold values from 0 to 32767
Outputs:
- subgrids: float32 [4, 8, 512, 1024], P('col', 'facet')
Inputs may be any that keep to these rules, and one draw needn't show every extreme that they name: `col_u`: offset in the image. `slot_col`: the subgrid's column is owner * 2 + this value. `slot_v`: offset in the image.
All inputs are finite; a program needn't handle non-finite values.
Results may differ from a plain program's by a relative error of at most 0.0003.
Values sent between devices are 32-bit elements; how exact they have to be, the bound alone decides.
A program may use at most 128 MiB of HBM per device.

v0:
```python
import math
import jax
import jax.numpy as jnp
from jax import lax
from jax.sharding import PartitionSpec as P

FS = 4096
SG = 512
COLS_DEV = 2
SLOTS = 1


def mulmod(first_factor, second_factor, modulus):
    upper = first_factor * (second_factor // 512) % modulus
    return (upper * 512 + first_factor * (second_factor % 512)) % modulus


def column_part(real_part, imag_part, shifted, table, col_u, img, count):
    turn = 2.0 * math.pi / img
    column_angle = mulmod(col_u[:, None], shifted[None, :], img).astype(jnp.float32) * turn
    cosine = jnp.cos(column_angle)[:, None, :]
    sine = jnp.sin(column_angle)[:, None, :]
    turned_real = real_part[None] * cosine + imag_part[None] * sine
    turned_imag = imag_part[None] * cosine - real_part[None] * sine
    local_rows = real_part.shape[0]
    width = real_part.shape[1]
    stacked = jnp.stack([turned_real, turned_imag]).reshape(-1, width)
    product = jnp.dot(
        stacked, table, precision=lax.Precision.HIGHEST, preferred_element_type=jnp.float32
    )
    product = product.reshape(2, count, local_rows, 2 * SG)
    from_real = product[0]
    from_imag = product[1]
    real_out = from_real[..., :SG] + from_imag[..., SG:]
    imag_out = from_imag[..., :SG] - from_real[..., SG:]
    return jnp.concatenate([real_out, imag_out], axis=-1)


def slot_term(owned, row_cells, img, column, shift_v):
    turn = 2.0 * math.pi / img
    v_cells = (shift_v + jnp.arange(SG, dtype=jnp.int32)) % img
    angle = mulmod(v_cells[:, None], row_cells[None, :], img).astype(jnp.float32) * turn
    cosine = jnp.cos(angle)
    sine = jnp.sin(angle)
    chosen = lax.dynamic_index_in_dim(owned, column, 0, keepdims=False)
    first = jnp.dot(
        cosine, chosen, precision=lax.Precision.HIGHEST, preferred_element_type=jnp.float32
    )
    second = jnp.dot(
        sine, chosen, precision=lax.Precision.HIGHEST, preferred_element_type=jnp.float32
    )
    real_out = first[:, :SG] + second[:, SG:]
    imag_out = first[:, SG:] - second[:, :SG]
    return jnp.concatenate([real_out, imag_out], axis=-1)


def per_device(facets, facet_x, facet_y, col_u, slot_col, slot_v):
    width = facets.shape[-1]
    band_rows = facets.shape[2]
    img = FS * lax.axis_size("facet")
    turn = 2.0 * math.pi / img
    x_start = lax.axis_index("col") * width
    real_part = facets[:, 0, :, 0, :].reshape(-1, width)
    imag_part = facets[:, 0, :, 1, :].reshape(-1, width)
    shifted = (facet_x[0] + x_start + jnp.arange(width, dtype=jnp.int32)) % img
    u_cells = jnp.arange(SG, dtype=jnp.int32)
    table_angle = mulmod(u_cells[None, :], shifted[:, None], img).astype(jnp.float32) * turn
    table = jnp.concatenate([jnp.cos(table_angle), jnp.sin(table_angle)], axis=1)
    owned = lax.psum_scatter(
        column_part(
            real_part, imag_part, shifted, table, col_u, img, COLS_DEV * lax.axis_size("col")
        ),
        "col",
        scatter_dimension=0,
        tiled=True,
    )
    total_rows = owned.shape[1]
    row_ids = jnp.arange(total_rows, dtype=jnp.int32)
    y_start = jnp.where(row_ids // band_rows == 0, facet_y[0], facet_y[1])
    row_cells = (y_start + row_ids % band_rows) % img
    scale = 1.0 / math.sqrt(2.0 * FS * band_rows * lax.axis_size("facet"))
    owner_cols = slot_col[0]
    owner_shift = slot_v[0]
    merged = lax.psum(owned, "facet")

    def own_slot(slot_id):
        return slot_term(merged, row_cells, img, owner_cols[slot_id], owner_shift[slot_id])

    first_slot = lax.axis_index("facet") * SLOTS
    summed = lax.map(own_slot, first_slot + jnp.arange(SLOTS, dtype=jnp.int32))
    return (summed * scale)[None]


def solution(mesh):
    placed = (
        P(None, "facet", None, None, "col"),
        P("facet"),
        P(),
        P(),
        P("col", None),
        P("col", None),
    )
    return jax.shard_map(
        per_device,
        mesh=mesh,
        in_specs=placed,
        out_specs=P("col", "facet", None, None),
        check_vma=False,
    )
```

profile of v0, /device:TPU:0, one launch (start us, length us, event | category | flops | bytes accessed | tf_op | source)
XLA Modules:
  0.0 140.9 jit_solution(5407549524900106008)
XLA Ops:
  7.2 0.0 copy-start.3
  7.2 0.0 copy-start
  7.2 9.3 %fusion.16 = (f32[1024,512]{1,0:T(8,128)S(1)}, f32[1024,512]{1,0:T(8,128)S(1)}) fusion(s32[1024]{0:T(1024)S(1)} %get-tuple-element.42, s32[1024]{0:T(1024)S(1)} %get-tuple-element.43), kind=kLoop, calls=%fused_computation.29 | loop fusion | flops 14680064 | bytes 4202496 | tf_op jit(solution)/shard_map/cos | solution.py:68
  16.5 0.2 fusion.40
  16.8 0.3 fusion.62
  17.2 0.4 multiply_add_fusion
  17.6 0.4 pad_maximum_fusion
  18.0 10.6 %fusion = f32[768,1024]{1,0:T(8,128)S(1)} fusion(f32[768,1024]{1,0:T(8,128)S(1)} %bitcast.23, f32[1024,512]{1,0:T(8,128)S(1)} %get-tuple-element.39, f32[1024,512]{1,0:T(8,128)S(1)} %get-tuple-element.38), kind=kOutput, calls=%fused_computation | convolution fusion | flops 9664724992 | bytes 10485760 | tf_op jit(solution)/shard_map/dot_general | solution.py:28
  28.6 0.4 fusion.61
  29.0 0.3 slice_add_fusion.1
  29.4 1.3 pad_maximum_fusion.1
  30.7 0.0 reduce-scatter.2.cloned.1.call-update
  30.7 0.3 all-reduce.2.cloned.1.call-start
  31.0 0.6 constant_dynamic-slice_fusion
  33.5 0.6 fusion.63
  34.1 34.9 %reduce-scatter.2.cloned.1.call-done = f32[2,48,1024]{2,1,0:T(8,128)} async-done(((f32[8,48,1024]{2,1,0:T(8,128)}), f32[2,48,1024]{2,1,0:T(8,128)}) %reduce-scatter.2.cloned.1.call-update) | async-done | bytes 393232 | tf_op jit(solution)/shard_map/reduce_scatter | solution.py:69
  69.0 0.0 all-reduce.2.cloned.1.call-update
  69.0 1.2 and_select_fusion
  70.2 0.6 add_select_fusion.9
  70.9 54.4 %all-reduce.2.cloned.1.call-done = f32[2,48,1024]{2,1,0:T(8,128)} async-done(((f32[2,48,1024]{2,1,0:T(8,128)}), f32[2,48,1024]{2,1,0:T(8,128)}) %all-reduce.2.cloned.1.call-update) | async-done | bytes 393232 | tf_op jit(solution)/shard_map/psum | solution.py:84
  125.3 3.8 %fusion.25 = f32[512,1024]{1,0:T(8,128)S(1)} fusion(f32[2,48,1024]{2,1,0:T(8,128)} %all-reduce.2.cloned.1.call-done, s32[]{:T(128)S(6)} %select_n.215, s32[48]{0:T(128)S(1)} %get-tuple-element.44, s32[48]{0:T(128)S(1)} %get-tuple-element.45, s32[512]{0:T(512)S(1)} %add_select_fusion.9), kind=kOutput, calls=%fused_computation.48 | convolution fusion | flops 302678016 | bytes 2296196 | tf_op jit(solution)/shard_map/while/body/eval_jaxpr/dot_general | solution.py:46
  129.2 2.8 %fusion.23 = f32[512,1024]{1,0:T(8,128)S(1)} fusion(f32[2,48,1024]{2,1,0:T(8,128)S(1)} %copy-done.1, s32[]{:T(128)S(6)} %select_n.215, s32[48]{0:T(128)S(1)} %get-tuple-element.44, s32[48]{0:T(128)S(1)} %get-tuple-element.45, s32[512]{0:T(512)S(1)} %add_select_fusion.9), kind=kOutput, calls=%fused_computation.46 | convolution fusion | flops 302678016 | bytes 2296836 | tf_op jit(solution)/shard_map/while/body/eval_jaxpr/dot_general | solution.py:49
  132.0 0.5 fusion.14
  132.5 1.5 %maximum_multiply_fusion = f32[1,1,512,1024]{3,2,1,0:T(8,128)} fusion(f32[1,1,512,512]{3,2,1,0:T(8,128)S(1)} %get-tuple-element.18, f32[1,1,512,512]{3,2,1,0:T(8,128)S(1)} %get-tuple-element.17), kind=kLoop, calls=%fused_computation.17 | loop fusion | flops 1048576 | bytes 4194304 | tf_op jit(solution)/shard_map/mul | solution.py:91
  (14 shorter events, 0.1 us)
Async XLA Ops:
  6.5 62.5 %reduce-scatter.2.cloned.1.call-start = ((), (), s32[]{:S(2)}) async-start(), calls=%async_computation.1 | async-start | bytes 1966080 | tf_op jit(solution)/shard_map/reduce_scatter | solution.py:69
  7.2 9.3 %copy-start.3 = (s32[8]{0:T(128)S(1)}, s32[8]{0:T(128)}, u32[]{:S(2)}) copy-start(s32[8]{0:T(128)} %param.9) | copy-start | bytes 100
  7.2 9.6 %copy-start = (f32[2,1,24,2,1024]{4,3,2,1,0:T(2,128)S(1)}, f32[2,1,24,2,1024]{4,3,2,1,0:T(2,128)}, u32[]{:S(2)}) copy-start(f32[2,1,24,2,1024]{4,3,2,1,0:T(2,128)} %param.6) | copy-start | bytes 1179652
  29.3 1.6 %copy-start.4 = (s32[1,8]{1,0:T(1,128)S(1)}, s32[1,8]{1,0:T(1,128)}, u32[]{:S(2)}) copy-start(s32[1,8]{1,0:T(1,128)} %param.10) | copy-start | bytes 100
  29.4 1.6 %copy-start.5 = (s32[1,8]{1,0:T(1,128)S(1)}, s32[1,8]{1,0:T(1,128)}, u32[]{:S(2)}) copy-start(s32[1,8]{1,0:T(1,128)} %param.11) | copy-start | bytes 100
  29.4 4.1 %copy-start.2 = (s32[2]{0:T(128)S(1)}, s32[2]{0:T(128)}, u32[]{:S(2)}) copy-start(s32[2]{0:T(128)} %param.8) | copy-start | bytes 28
  30.7 94.6 %all-reduce.2.cloned.1.call-start = ((), (), s32[]{:S(2)}) async-start(), calls=%async_computation.2 | async-start | bytes 786432 | tf_op jit(solution)/shard_map/psum | solution.py:84
  125.3 3.8 %copy-start.1 = (f32[2,48,1024]{2,1,0:T(8,128)S(1)}, f32[2,48,1024]{2,1,0:T(8,128)}, u32[]{:S(2)}) copy-start(f32[2,48,1024]{2,1,0:T(8,128)} %all-reduce.2.cloned.1.call-done) | copy-start | bytes 1179652
Sparse Core Ops, SparseCore 0:
  30.8 38.1 reduce-scatter.1
  72.1 53.2 all-reduce.1
where the time goes:
time: 141 us
  waiting for transfers between devices  89.4 us (63%)
  matrix products  17.2 us (12%)
  between operations  16.2 us (11%)
  other arithmetic  15.9 us (11%)
  local copies, waits for them, and re-layouts  1.98 us (1%)
    psum x1, waiting for transfers between devices, per_device(): merged = lax.psum(owned, 'facet')  54.4 us
    reduce_scatter x1, waiting for transfers between devices, per_device(): lax.psum_scatter(column_part(real_part, imag_part, shifted, table, col_u,...  34.9 us
    dot_general x1, matrix products, column_part(): jnp.dot(stacked, table, precision=lax.Precision.HIGHEST, preferred_elemen...  10.6 us
    cos x1, other arithmetic, per_device(): jnp.cos(table_angle)  9.29 us
    dot_general x1, matrix products, slot_term(): jnp.dot(cosine, chosen, precision=lax.Precision.HIGHEST, preferred_elemen...  3.81 us
    dot_general x1, matrix products, slot_term(): jnp.dot(sine, chosen, precision=lax.Precision.HIGHEST, preferred_element_...  2.82 us
  transfers between devices with their start and end apart: 2, of which 2 were waited for; matrix products, arithmetic and copies ran while one was open for 2% of the time, Pallas kernels for 0%

commit v1 on v0

--- a/solution.py
+++ b/solution.py
@@ -81,7 +81,9 @@
     scale = 1.0 / math.sqrt(2.0 * FS * band_rows * lax.axis_size("facet"))
     owner_cols = slot_col[0]
     owner_shift = slot_v[0]
-    merged = lax.psum(owned, "facet")
+    merged = owned
+    for hop in (1, 2, 4):
+        merged = merged + lax.ppermute(merged, "facet", [(dev, dev ^ hop) for dev in range(8)])
 
     def own_slot(slot_id):
         return slot_term(merged, row_cells, img, owner_cols[slot_id], owner_shift[slot_id])

time: 141 us -> 109 us (0.77)
  waiting for transfers between devices: 89.4 us -> 53.6 us
  starting transfers between devices: 0.26 us -> 3.1 us
    psum x1 -> x0, waiting for transfers between devices: 54.4 us -> none  [per_device(): merged = lax.psum(owned, 'facet')]
    ppermute x0 -> x3, waiting for transfers between devices: none -> 15.3 us  [per_device(): lax.ppermute(merged, 'facet', [(dev, dev ^ hop) for dev in range(8)])]
    reduce_scatter x1, waiting for transfers between devices: 34.9 us -> 38.3 us  [per_device(): lax.psum_scatter(column_part(real_part, imag_part, shifted, table, col_u,...]
    ppermute x0 -> x3, starting transfers between devices: none -> 3.1 us  [per_device(): lax.ppermute(merged, 'facet', [(dev, dev ^ hop) for dev in range(8)])]
  transfers between devices with their start and end apart: 2 -> 4, of which waited for: 2 -> 4; matrix products, arithmetic and copies ran while one was open for 2% -> 3% of each run, Pallas kernels for 0% -> 0%
where the time goes in v1:
time: 109 us; the launch traced here: 108 us
  waiting for transfers between devices  53.6 us (49%)
  other arithmetic  17 us (16%)
  matrix products  16.4 us (15%)
  between operations  16.1 us (15%)
  starting transfers between devices  3.1 us (3%)
  local copies, waits for them, and re-layouts  2.02 us (2%)
    reduce_scatter x1, waiting for transfers between devices, per_device(): lax.psum_scatter(column_part(real_part, imag_part, shifted, table, col_u,...  38.3 us
    ppermute x3, waiting for transfers between devices, per_device(): lax.ppermute(merged, 'facet', [(dev, dev ^ hop) for dev in range(8)])  15.3 us
    dot_general x1, matrix products, column_part(): jnp.dot(stacked, table, precision=lax.Precision.HIGHEST, preferred_elemen...  10.6 us
    cos x1, other arithmetic, per_device(): jnp.cos(table_angle)  9.29 us
    ppermute x3, starting transfers between devices, per_device(): lax.ppermute(merged, 'facet', [(dev, dev ^ hop) for dev in range(8)])  3.1 us
    dot_general x1, matrix products, slot_term(): jnp.dot(sine, chosen, precision=lax.Precision.HIGHEST, preferred_element_...  3.05 us
    dot_general x1, matrix products, slot_term(): jnp.dot(cosine, chosen, precision=lax.Precision.HIGHEST, preferred_elemen...  2.82 us
  transfers between devices with their start and end apart: 4, of which 4 were waited for; matrix products, arithmetic and copies ran while one was open for 3% of the time, Pallas kernels for 0%

profile of v1, /device:TPU:0, one launch (start us, length us, event | category | flops | bytes accessed | tf_op | source)
XLA Modules:
  0.0 108.3 jit_solution(2230050056031637530)
XLA Ops:
  7.2 9.3 %fusion.16 = (f32[1024,512]{1,0:T(8,128)S(1)}, f32[1024,512]{1,0:T(8,128)S(1)}) fusion(s32[1024]{0:T(1024)S(1)} %get-tuple-element.42, s32[1024]{0:T(1024)S(1)} %get-tuple-element.43), kind=kLoop, calls=%fused_computation.29 | loop fusion | flops 14680064 | bytes 4202496 | tf_op jit(solution)/shard_map/cos | solution.py:68
  16.5 0.2 fusion.39
  16.8 0.3 fusion.61
  17.2 0.4 multiply_add_fusion
  17.6 0.4 pad_maximum_fusion
  18.0 10.6 %fusion = f32[768,1024]{1,0:T(8,128)S(1)} fusion(f32[768,1024]{1,0:T(8,128)S(1)} %bitcast.22, f32[1024,512]{1,0:T(8,128)S(1)} %get-tuple-element.39, f32[1024,512]{1,0:T(8,128)S(1)} %get-tuple-element.38), kind=kOutput, calls=%fused_computation | convolution fusion | flops 9664724992 | bytes 10485760 | tf_op jit(solution)/shard_map/dot_general | solution.py:28
  28.6 0.4 fusion.60
  29.0 0.3 slice_add_fusion.1
  29.3 1.3 %pad_maximum_fusion.1 = f32[8,48,1024]{2,1,0:T(8,128)} fusion(f32[8,48,512]{2,1,0:T(8,128)S(1)} %get-tuple-element.20, f32[8,48,512]{2,1,0:T(8,128)S(1)} %get-tuple-element.19), kind=kLoop, calls=%fused_computation.21 | loop fusion | flops 393216 | bytes 3145728 | tf_op jit(solution)/shard_map/concatenate | solution.py:36
  30.7 38.3 %reduce-scatter.2.cloned.1.call-done = f32[2,48,1024]{2,1,0:T(8,128)} async-done(((f32[8,48,1024]{2,1,0:T(8,128)}), f32[2,48,1024]{2,1,0:T(8,128)}) %reduce-scatter.2.cloned.1.call-update) | async-done | bytes 393232 | tf_op jit(solution)/shard_map/reduce_scatter | solution.py:69
  69.0 1.9 %collective-permute-done = f32[2,48,1024]{2,1,0:T(8,128)S(1)} collective-permute-done((f32[2,48,1024]{2,1,0:T(8,128)}, f32[2,48,1024]{2,1,0:T(8,128)S(1)}, u32[]{:S(2)}, u32[]{:S(2)}) %collective-permute-start) | collective-permute-done | bytes 393248 | tf_op jit(solution)/shard_map/ppermute | solution.py:86
  70.9 1.1 add.286
  71.9 1.5 %collective-permute-start.1 = (f32[2,48,1024]{2,1,0:T(8,128)S(1)}, f32[2,48,1024]{2,1,0:T(8,128)S(1)}, u32[]{:S(2)}, u32[]{:S(2)}) collective-permute-start(f32[2,48,1024]{2,1,0:T(8,128)S(1)} %add.286), channel_id=1, source_target_pairs={{0,8},{4,12},{8,0},{12,4},{16,24},{20,28},{24,16},{28,20},{1,9},{5... | collective-permute-start | bytes 1179656 | tf_op jit(solution)/shard_map/ppermute | solution.py:86
  73.5 9.7 %collective-permute-done.1 = f32[2,48,1024]{2,1,0:T(8,128)S(1)} collective-permute-done((f32[2,48,1024]{2,1,0:T(8,128)S(1)}, f32[2,48,1024]{2,1,0:T(8,128)S(1)}, u32[]{:S(2)}, u32[]{:S(2)}) %collective-permute-start.1) | collective-permute-done | bytes 393248 | tf_op jit(solution)/shard_map/ppermute | solution.py:86
  83.2 1.5 %collective-permute-start.2 = (f32[2,48,1024]{2,1,0:T(8,128)S(1)}, f32[2,48,1024]{2,1,0:T(8,128)S(1)}, u32[]{:S(2)}, u32[]{:S(2)}) collective-permute-start(f32[2,48,1024]{2,1,0:T(8,128)S(1)} %add.287), channel_id=1, source_target_pairs={{0,16},{4,20},{8,24},{12,28},{16,0},{20,4},{24,8},{28,12},{1,17},{... | collective-permute-start | bytes 1179656 | tf_op jit(solution)/shard_map/ppermute | solution.py:86
  84.8 0.7 constant_dynamic-slice_fusion
  87.4 0.6 fusion.62
  88.0 1.2 %and_select_fusion = (s32[48]{0:T(128)S(1)}, s32[48]{0:T(128)S(1)}) fusion(s32[]{:T(128)} %bitcast.2, s32[]{:T(128)} %bitcast.1), kind=kLoop, calls=%fused_computation.89 | loop fusion | flops 2160 | bytes 392 | tf_op jit(solution)/shard_map/while/body/eval_jaxpr/jit(remainder)/select_n | solution.py:15
  89.2 0.7 add_select_fusion.9
  89.9 3.7 %collective-permute-done.2 = f32[2,48,1024]{2,1,0:T(8,128)S(1)} collective-permute-done((f32[2,48,1024]{2,1,0:T(8,128)S(1)}, f32[2,48,1024]{2,1,0:T(8,128)S(1)}, u32[]{:S(2)}, u32[]{:S(2)}) %collective-permute-start.2) | collective-permute-done | bytes 393248 | tf_op jit(solution)/shard_map/ppermute | solution.py:86
  93.6 2.8 %fusion.25 = f32[512,1024]{1,0:T(8,128)S(1)} fusion(s32[48]{0:T(128)S(1)} %get-tuple-element.44, s32[48]{0:T(128)S(1)} %get-tuple-element.45, s32[512]{0:T(512)S(1)} %add_select_fusion.9, f32[2,48,1024]{2,1,0:T(8,128)S(1)} %collective-permute-done.2, s32[]{:T(128)S(6)} %select_n.215, f32[2,48,1024]{2,1,0:T(8,128)S(1)} %add.287), kind=kOutput, calls=%fused_computation.48 | convolution fusion | flops 302727168 | bytes 2493444 | tf_op jit(solution)/shard_map/while/body/eval_jaxpr/dot_general | solution.py:46
  96.4 3.1 %fusion.23 = f32[512,1024]{1,0:T(8,128)S(1)} fusion(s32[48]{0:T(128)S(1)} %get-tuple-element.44, s32[48]{0:T(128)S(1)} %get-tuple-element.45, s32[512]{0:T(512)S(1)} %add_select_fusion.9, f32[2,48,1024]{2,1,0:T(8,128)S(1)} %collective-permute-done.2, s32[]{:T(128)S(6)} %select_n.215, f32[2,48,1024]{2,1,0:T(8,128)S(1)} %add.287), kind=kOutput, calls=%fused_computation.46 | convolution fusion | flops 302727168 | bytes 2493444 | tf_op jit(solution)/shard_map/while/body/eval_jaxpr/dot_general | solution.py:49
  99.5 0.5 fusion.14
  100.0 1.5 %maximum_multiply_fusion = f32[1,1,512,1024]{3,2,1,0:T(8,128)} fusion(f32[1,1,512,512]{3,2,1,0:T(8,128)S(1)} %get-tuple-element.18, f32[1,1,512,512]{3,2,1,0:T(8,128)S(1)} %get-tuple-element.17), kind=kLoop, calls=%fused_computation.17 | loop fusion | flops 1048576 | bytes 4194304 | tf_op jit(solution)/shard_map/mul | solution.py:93
  (17 shorter events, 0.2 us)
Async XLA Ops:
  6.5 62.4 %reduce-scatter.2.cloned.1.call-start = ((), (), s32[]{:S(2)}) async-start(), calls=%async_computation.1 | async-start | bytes 1966080 | tf_op jit(solution)/shard_map/reduce_scatter | solution.py:69
  7.2 9.3 %copy-start.2 = (s32[8]{0:T(128)S(1)}, s32[8]{0:T(128)}, u32[]{:S(2)}) copy-start(s32[8]{0:T(128)} %param.9) | copy-start | bytes 100
  7.2 9.6 %copy-start = (f32[2,1,24,2,1024]{4,3,2,1,0:T(2,128)S(1)}, f32[2,1,24,2,1024]{4,3,2,1,0:T(2,128)}, u32[]{:S(2)}) copy-start(f32[2,1,24,2,1024]{4,3,2,1,0:T(2,128)} %param.6) | copy-start | bytes 1179652
  30.6 54.1 %copy-start.3 = (s32[1,8]{1,0:T(1,128)S(1)}, s32[1,8]{1,0:T(1,128)}, u32[]{:S(2)}) copy-start(s32[1,8]{1,0:T(1,128)} %param.10) | copy-start | bytes 100
  30.6 54.1 %copy-start.4 = (s32[1,8]{1,0:T(1,128)S(1)}, s32[1,8]{1,0:T(1,128)}, u32[]{:S(2)}) copy-start(s32[1,8]{1,0:T(1,128)} %param.11) | copy-start | bytes 100
  30.6 56.8 %copy-start.1 = (s32[2]{0:T(128)S(1)}, s32[2]{0:T(128)}, u32[]{:S(2)}) copy-start(s32[2]{0:T(128)} %param.8) | copy-start | bytes 28
  69.0 1.9 %collective-permute-start = (f32[2,48,1024]{2,1,0:T(8,128)}, f32[2,48,1024]{2,1,0:T(8,128)S(1)}, u32[]{:S(2)}, u32[]{:S(2)}) collective-permute-start(f32[2,48,1024]{2,1,0:T(8,128)} %reduce-scatter.2.cloned.1.call-done), channel_id=1, source_target_pairs={{0,4},{4,0},{8,12},{12,8},{16,20},{20,16},{24,28},{28,24},{1,5},{5... | collective-permute-start | bytes 1179656 | tf_op jit(solution)/shard_map/ppermute | solution.py:86
  71.9 11.2 %collective-permute-start.1 = (f32[2,48,1024]{2,1,0:T(8,128)S(1)}, f32[2,48,1024]{2,1,0:T(8,128)S(1)}, u32[]{:S(2)}, u32[]{:S(2)}) collective-permute-start(f32[2,48,1024]{2,1,0:T(8,128)S(1)} %add.286), channel_id=1, source_target_pairs={{0,8},{4,12},{8,0},{12,4},{16,24},{20,28},{24,16},{28,20},{1,9},{5... | collective-permute-start | bytes 1179656 | tf_op jit(solution)/shard_map/ppermute | solution.py:86
  83.2 10.4 %collective-permute-start.2 = (f32[2,48,1024]{2,1,0:T(8,128)S(1)}, f32[2,48,1024]{2,1,0:T(8,128)S(1)}, u32[]{:S(2)}, u32[]{:S(2)}) collective-permute-start(f32[2,48,1024]{2,1,0:T(8,128)S(1)} %add.287), channel_id=1, source_target_pairs={{0,16},{4,20},{8,24},{12,28},{16,0},{20,4},{24,8},{28,12},{1,17},{... | collective-permute-start | bytes 1179656 | tf_op jit(solution)/shard_map/ppermute | solution.py:86
Sparse Core Ops, SparseCore 0:
  30.8 38.1 reduce-scatter.1
